TPU v7x, 128 devices: a whole 4x4x4 slice. The times are simulated.
128 devices in a mesh: frame: 32 (over x, y, z_lo), row: 4 (over z_hi, core).
Axes of the slice: x: 4, y: 4, z: 4 (z_hi: 2, z_lo: 2; z = z_hi * 2 + z_lo), core: 2. Of those that a mesh axis runs over, the one named last changes fastest.
Arguments:
- query_pre: bfloat16 [2240, 32, 16, 128], P(None, 'frame', 'row'), may hold values from -6 to 6
- key_pre: bfloat16 [2240, 32, 16, 128], P(None, 'frame', 'row'), may hold values from -80 to 80
- values: bfloat16 [2240, 32, 16, 128], P(None, 'frame', 'row'), may hold values from -1 to 2
- cotangent: bfloat16 [2240, 32, 16, 128], P(None, 'frame', 'row'), may hold values from -3072 to 3072
- kernel: bfloat16 [3, 3, 2240], replicated, may hold values from -0.29882812 to 0.59765625
Outputs:
- grad_query: bfloat16 [2240, 32, 16, 128], P(None, 'frame', 'row')
- grad_key: bfloat16 [2240, 32, 16, 128], P(None, 'frame', 'row')
- grad_values: bfloat16 [2240, 32, 16, 128], P(None, 'frame', 'row')
All inputs are finite; a program needn't handle non-finite values.
Results may differ from a plain program's by a relative error of at most 0.008.
Values may be sent and summed in bfloat16 or wider, within the bound.
A program may use at most 128 MiB of HBM per device.

v0:
```python
import jax
import jax.numpy as jnp
from jax import lax
from jax.sharding import PartitionSpec as P

HD = 32
denominator_eps = 0.001


def extended(array, sides, width):
    for axis, dim in sides:
        size, length = (lax.axis_size(axis), array.shape[dim])
        up = [(i, (i + 1) % size) for i in range(size - 1)]
        down = [(j, i) for i, j in up]
        last = lax.slice_in_dim(array, length - width, length, axis=dim)
        leading = lax.slice_in_dim(array, 0, width, axis=dim)
        before = lax.ppermute(last, axis, up)
        after = lax.ppermute(leading, axis, down)
        array = jnp.concatenate([before, array, after], axis=dim)
    return array


def conv_taps(padded, weights, flipped, row_count, col_count):
    summed = None
    for tap_row in range(3):
        for tap_col in range(3):
            start_row = 2 - tap_row if flipped else tap_row
            start_col = 2 - tap_col if flipped else tap_col
            window = padded[
                :, :, start_row : start_row + row_count, start_col : start_col + col_count
            ]
            tap_term = weights[tap_row, tap_col][:, None, None, None] * window
            summed = tap_term if summed is None else summed + tap_term
    return summed


def pad_columns(field):
    return jnp.pad(field, ((0, 0), (0, 0), (0, 0), (1, 1)))


def shards(query_pre, key_pre, values, cotangent, kernel):
    highest = lax.Precision.HIGHEST
    channels, frames, row_count, col_count = values.shape
    head_count = channels // HD
    tokens_dev = frames * row_count * col_count
    all_tokens = tokens_dev * lax.axis_size("frame") * lax.axis_size("row")
    flat = (head_count, HD, tokens_dev)
    weights = kernel.astype(jnp.float32)
    value_ext = extended(values, (("row", 2),), 1)
    value_pad = pad_columns(value_ext.astype(jnp.float32))
    mixed = conv_taps(value_pad, weights, False, row_count, col_count).reshape(flat)
    key_act = jax.nn.relu(key_pre.astype(jnp.float32)).reshape(flat)
    query_act = jax.nn.relu(query_pre.astype(jnp.float32)).reshape(flat)
    local_state = jnp.einsum("hjt,het->hje", key_act, mixed, precision=highest)
    local_sum = jnp.sum(key_act, axis=2)
    state, key_sum = lax.psum((local_state, local_sum), ("frame", "row"))
    denom = (
        jnp.einsum("hj,hjt->ht", key_sum, query_act, precision=highest)
        + denominator_eps * all_tokens
    )
    numer = jnp.einsum("hje,hjt->het", state, query_act, precision=highest)
    output = numer / denom[:, None, :]
    grad_out = cotangent.astype(jnp.float32).reshape(flat)
    grad_num = grad_out / denom[:, None, :]
    grad_den = -jnp.sum(grad_out * output, axis=1) / denom
    local_gstate = jnp.einsum("hjt,het->hje", query_act, grad_num, precision=highest)
    local_gsum = jnp.einsum("hjt,ht->hj", query_act, grad_den, precision=highest)
    grad_state, grad_sum = lax.psum((local_gstate, local_gsum), ("frame", "row"))
    grad_qact = (
        jnp.einsum("hje,het->hjt", state, grad_num, precision=highest)
        + key_sum[:, :, None] * grad_den[:, None, :]
    )
    grad_query = (
        jnp.where(query_pre.reshape(flat) > 0, grad_qact, 0.0)
        .astype(jnp.bfloat16)
        .reshape(values.shape)
    )
    grad_mixed = jnp.einsum("hje,hjt->het", grad_state, key_act, precision=highest)
    grad_kact = (
        jnp.einsum("hje,het->hjt", grad_state, mixed, precision=highest) + grad_sum[:, :, None]
    )
    grad_key = (
        jnp.where(key_pre.reshape(flat) > 0, grad_kact, 0.0)
        .astype(jnp.bfloat16)
        .reshape(values.shape)
    )
    grad_grid = grad_mixed.reshape(channels, frames, row_count, col_count)
    grad_ext = extended(grad_grid.astype(jnp.bfloat16), (("row", 2),), 1).astype(grad_grid.dtype)
    grad_values = conv_taps(pad_columns(grad_ext), weights, True, row_count, col_count).astype(
        jnp.bfloat16
    )
    return (grad_query, grad_key, grad_values)


def solution(mesh):
    return jax.shard_map(
        shards,
        mesh=mesh,
        in_specs=(
            P(None, "frame", "row", None),
            P(None, "frame", "row", None),
            P(None, "frame", "row", None),
            P(None, "frame", "row", None),
            P(),
        ),
        out_specs=(
            P(None, "frame", "row", None),
            P(None, "frame", "row", None),
            P(None, "frame", "row", None),
        ),
        check_vma=False,
    )
```

profile of v0, /device:TPU:1, one launch (start us, length us, event | category | flops | bytes accessed | tf_op | source)
XLA Modules:
  0.0 554.9 jit_solution(3331773693273662485)
XLA Ops:
  7.2 0.0 all-reduce.5.cloned.1.call-start
  7.2 4.5 fusion.36
  11.7 0.9 copy.42
  12.6 3.4 collective-permute-start.1
  16.0 0.9 copy.41
  16.9 5.5 collective-permute-start
  22.4 5.1 reshape.172
  27.6 18.0 %fusion.30 = (f32[2240]{0:T(1024)S(1)}, f32[2240,1,4,128]{3,2,1,0:T(4,128)}) fusion(bf16[2240,1,4,128]{3,2,1,0:T(4,128)(2,1)S(1)} %copy-done.2), kind=kLoop, calls=%fused_computation.59 | loop fusion | flops 3438400 | bytes 6890240 | tf_op jit(solution)/shard_map/reduce_sum | solution.py:55
  45.5 6.3 %reshape.164 = f32[70,32,512]{2,1,0:T(8,128)} reshape(f32[2240,1,4,128]{3,2,1,0:T(4,128)} %get-tuple-element.26) | data formatting | bytes 9175040 | tf_op jit(solution)/shard_map/reshape | solution.py:52
  51.9 0.8 slice_reduce_fusion.8
  52.7 4.6 convert_maximum_fusion
  57.3 6.3 %reshape.168 = f32[70,32,512]{2,1,0:T(8,128)} reshape(f32[2240,1,4,128]{3,2,1,0:T(4,128)} %convert_maximum_fusion) | data formatting | bytes 9175040 | tf_op jit(solution)/shard_map/reshape | solution.py:53
  63.6 0.1 reduce_sum.21
  63.7 65.3 %psum.29 = f32[70,32]{1,0:T(8,128)S(1)} all-reduce(f32[70,32]{1,0:T(8,128)S(1)} %reduce_sum.21), channel_id=1, replica_groups=mesh['frame'=32,'row'=4] {'frame','row'}, use_global_device_ids=true, to_apply=%region_2.3 | all-reduce | flops 2240 | bytes 17920 | tf_op jit(solution)/shard_map/psum | solution.py:56
  129.1 4.8 fusion.33
  133.8 0.7 copy-done.5
  134.5 0.0 copy-start.3
  134.5 8.0 %fusion.29 = f32[70,32,32]{2,1,0:T(8,128)} fusion(f32[70,32,512]{2,1,0:T(8,128)S(1)} %copy-done, f32[70,32,512]{2,1,0:T(8,128)} %reshape.172, f32[70,512]{1,0:T(8,128)S(1)} %bitcast_add_fusion), kind=kOutput, calls=%fused_computation.56 | convolution fusion | flops 441548800 | bytes 9605120 | tf_op jit(solution)/shard_map/hjt,het->hje/dot_general | solution.py:66
  142.5 0.0 copy-done.9
  142.5 1.5 broadcast_compare_fusion.1
  144.1 0.0 collective-permute-done.1
  144.1 5.7 %copy.25 = bf16[2240,1,1,128]{3,2,1,0:T(2,128)(2,1)S(1)} copy(bf16[2240,1,1,128]{3,0,2,1:T(8,128)(2,1)} %collective-permute-done.1) | data formatting | bytes 1146880 | tf_op jit(solution)/shard_map/ppermute | solution.py:18
  149.8 0.0 collective-permute-done
  149.8 5.9 %copy.24 = bf16[2240,1,1,128]{3,2,1,0:T(2,128)(2,1)S(1)} copy(bf16[2240,1,1,128]{3,0,2,1:T(8,128)(2,1)} %collective-permute-done) | data formatting | bytes 1146880 | tf_op jit(solution)/shard_map/ppermute | solution.py:17
  155.8 0.0 copy-done.1
  155.8 0.0 copy-start.18
  155.8 0.0 copy-start.20
  155.8 0.0 copy-start.22
  155.8 3.6 maximum_convert_fusion
  159.5 41.7 %fusion.8 = f32[2240,1,4,128]{3,2,1,0:T(4,128)} fusion(f32[2240,1,6,128]{3,2,1,0:T(8,128)S(1)} %maximum_convert_fusion, f32[2240]{0:T(1024)S(1)} %get-tuple-element.13, f32[2240]{0:T(1024)S(1)} %get-tuple-element.14, f32[2240]{0:T(1024)S(1)} %get-tuple-element.15, f32[2240]{0:T(1024)S(1)} %get-tuple-element.16, f32[2240]{0:T(1024)S(1)} %get-tuple-element.17, ...), kind=kLoop, calls=%fused_computation.20 | loop fusion | flops 19496960 | bytes 27635712 | tf_op jit(solution)/shard_map/add | solution.py:33
  201.2 6.3 %reshape.165 = f32[70,32,512]{2,1,0:T(8,128)} reshape(f32[2240,1,4,128]{3,2,1,0:T(4,128)} %fusion.8) | data formatting | bytes 9175040 | tf_op jit(solution)/shard_map/reshape | solution.py:51
  207.5 9.0 %fusion.37 = f32[70,32,32]{2,1,0:T(8,128)} fusion(f32[70,32,512]{2,1,0:T(8,128)} %reshape.164, f32[70,32,512]{2,1,0:T(8,128)} %reshape.165), kind=kOutput, calls=%fused_computation.78 | convolution fusion | flops 440401920 | bytes 9461760 | tf_op jit(solution)/shard_map/hjt,het->hje/dot_general | solution.py:54
  216.5 0.0 all-reduce.5.cloned.1.call-update
  216.5 2.5 broadcast_compare_fusion
  219.0 3.3 gt.13
  222.3 4.8 gt.15
  227.1 138.8 %all-reduce.5.cloned.1.call-done = (f32[70,32,32]{2,1,0:T(8,128)}, f32[70,32,32]{2,1,0:T(8,128)}) async-done(((f32[70,32,32]{2,1,0:T(8,128)}, f32[70,32,32]{2,1,0:T(8,128)}), (f32[70,32,32]{2,1,0:T(8,128)}, f32[70,32,32]{2,1,0:T(8,128)})) %all-reduce.5.cloned.1.call-update) | async-done | bytes 573456 | tf_op jit(solution)/shard_map/psum | solution.py:56
  365.9 8.2 %multiply_reduce_fusion = f32[70,512]{1,0:T(8,128)S(1)} fusion(f32[70,32,512]{2,1,0:T(8,128)} %reshape.172, f32[70,32,32]{2,1,0:T(8,128)} %get-tuple-element.21, f32[70,32,512]{2,1,0:T(8,128)} %reshape.168, f32[70,512]{1,0:T(8,128)S(1)} %copy-done.10), kind=kOutput, calls=%fused_computation.50 | convolution fusion | flops 443806720 | bytes 9748480 | tf_op jit(solution)/shard_map/hje,hjt->het/dot_general | solution.py:61
  374.1 0.7 negate_divide_fusion
  374.8 0.0 slice-done.3
  374.9 5.2 convolution_convert_fusion
  380.0 4.1 convert_element_type.73
  384.2 0.0 copy-start.7
  384.2 0.0 copy-start.8
  384.2 0.0 copy-start.11
  384.2 0.0 copy-start.25
  384.2 1.7 fusion.35
  385.9 0.9 copy.44
  386.8 2.9 collective-permute-start.3
  389.7 0.0 slice-start
  389.7 0.9 copy.43
  390.6 4.4 collective-permute-start.2
  395.1 8.6 %select_convert_fusion.1 = bf16[70,32,512]{2,1,0:T(8,128)(2,1)} fusion(pred[70,32,512]{2,1,0:T(32,128)(4,1)S(1)} %copy-done.7, f32[70,512]{1,0:T(8,128)S(1)} %copy-done.8, f32[70,32]{1,0:T(8,128)S(1)} %psum.29, f32[70,32,32]{2,1,0:T(8,128)S(1)} %copy-done.25, f32[70,32,512]{2,1,0:T(8,128)} %reshape.172, f32[70,512]{1,0:T(8,128)S(1)} %copy-done.11), kind=kOutput, calls=%fused_computation.49 | convolution fusion | flops 446136320 | bytes 8610560 | tf_op jit(solution)/shard_map/hje,het->hjt/dot_general | solution.py:70
  403.7 4.1 fusion.31
  407.7 5.1 reshape.169
  412.9 64.3 %psum.31 = f32[70,32]{1,0:T(8,128)S(1)} all-reduce(f32[70,32]{1,0:T(8,128)S(1)} %bitcast.32), channel_id=1, replica_groups=mesh['frame'=32,'row'=4] {'frame','row'}, use_global_device_ids=true, to_apply=%region_5.6 | all-reduce | flops 2240 | bytes 17920 | tf_op jit(solution)/shard_map/psum | solution.py:68
  477.2 8.6 %select_convert_fusion = bf16[70,32,512]{2,1,0:T(8,128)(2,1)} fusion(pred[70,32,512]{2,1,0:T(32,128)(4,1)S(1)} %gt.15, f32[70,32]{1,0:T(8,128)S(1)} %psum.31, f32[70,32,32]{2,1,0:T(8,128)} %get-tuple-element.22, f32[70,32,512]{2,1,0:T(8,128)} %reshape.165), kind=kOutput, calls=%fused_computation.48 | convolution fusion | flops 443842560 | bytes 8323840 | tf_op jit(solution)/shard_map/hje,het->hjt/dot_general | solution.py:80
  485.8 5.1 reshape.170
  490.9 0.0 collective-permute-done.3
  490.9 5.7 %copy.32 = bf16[2240,1,1,128]{3,2,1,0:T(2,128)(2,1)S(1)} copy(bf16[2240,1,1,128]{3,0,2,1:T(8,128)(2,1)} %collective-permute-done.3) | data formatting | bytes 1146880 | tf_op jit(solution)/shard_map/ppermute | solution.py:18
  496.7 0.0 collective-permute-done.2
  496.7 5.7 %copy.30 = bf16[2240,1,1,128]{3,2,1,0:T(2,128)(2,1)S(1)} copy(bf16[2240,1,1,128]{3,0,2,1:T(8,128)(2,1)} %collective-permute-done.2) | data formatting | bytes 1146880 | tf_op jit(solution)/shard_map/ppermute | solution.py:17
  502.5 3.6 maximum_convert_fusion.1
  506.2 41.7 %fusion.28 = bf16[2240,1,4,128]{3,2,1,0:T(4,128)(2,1)} fusion(f32[2240,1,6,128]{3,2,1,0:T(8,128)S(1)} %maximum_convert_fusion.1, f32[2240]{0:T(1024)S(1)} %get-tuple-element.13, f32[2240]{0:T(1024)S(1)} %get-tuple-element.14, f32[2240]{0:T(1024)S(1)} %copy-done.13, f32[2240]{0:T(1024)S(1)} %copy-done.15, f32[2240]{0:T(1024)S(1)} %copy-done.17, ...), kind=kLoop, calls=%fused_computation.53 | loop fusion | flops 20643840 | bytes 25341952 | tf_op jit(solution)/shard_map/convert_element_type | solution.py:89
  (52 shorter events, 0.1 us)
Async XLA Ops:
  7.2 358.7 %all-reduce.5.cloned.1.call-start = ((), (), s32[]{:S(2)}) async-start(), calls=%async_computation | async-start | bytes 4587520 | tf_op jit(solution)/shard_map/psum | solution.py:56
  12.6 14.9 %copy-start.2 = (bf16[2240,1,4,128]{3,2,1,0:T(4,128)(2,1)S(1)}, bf16[2240,1,4,128]{3,2,1,0:T(4,128)(2,1)}, u32[]{:S(2)}) copy-start(bf16[2240,1,4,128]{3,2,1,0:T(4,128)(2,1)} %param.6) | copy-start | bytes 6881284
  12.6 131.5 %collective-permute-start.1 = (bf16[2240,1,1,128]{3,0,2,1:T(8,128)(2,1)}, bf16[2240,1,1,128]{3,0,2,1:T(8,128)(2,1)}, u32[]{:S(2)}, u32[]{:S(2)}) collective-permute-start(bf16[2240,1,1,128]{3,0,2,1:T(8,128)(2,1)} %copy.42), channel_id=1, source_target_pairs={{1,0},{2,1},{3,2},{5,4},{6,5},{7,6},{9,8},{10,9},{11,10},{13,12},{... | collective-permute-start | bytes 1720328 | tf_op jit(solution)/shard_map/ppermute | solution.py:18
  16.9 132.9 %collective-permute-start = (bf16[2240,1,1,128]{3,0,2,1:T(8,128)(2,1)}, bf16[2240,1,1,128]{3,0,2,1:T(8,128)(2,1)}, u32[]{:S(2)}, u32[]{:S(2)}) collective-permute-start(bf16[2240,1,1,128]{3,0,2,1:T(8,128)(2,1)} %copy.41), channel_id=1, source_target_pairs={{0,1},{1,2},{2,3},{4,5},{5,6},{6,7},{8,9},{9,10},{10,11},{12,13},{... | collective-permute-start | bytes 1720328 | tf_op jit(solution)/shard_map/ppermute | solution.py:17
  45.5 6.3 %copy-start.24 = (bf16[3,3,2240]{2,1,0:T(4,128)(2,1)S(1)}, bf16[3,3,2240]{2,1,0:T(4,128)(2,1)}, u32[]{:S(2)}) copy-start(bf16[3,3,2240]{2,1,0:T(4,128)(2,1)} %param.9) | copy-start | bytes 120964
  52.7 106.8 %copy-start.12 = (f32[2240]{0:T(1024)}, f32[2240]{0:T(1024)S(1)}, u32[]{:S(2)}) copy-start(f32[2240]{0:T(1024)S(1)} %get-tuple-element.15) | copy-start | bytes 26884
  52.7 106.8 %copy-start.14 = (f32[2240]{0:T(1024)}, f32[2240]{0:T(1024)S(1)}, u32[]{:S(2)}) copy-start(f32[2240]{0:T(1024)S(1)} %get-tuple-element.16) | copy-start | bytes 26884
  52.7 106.8 %copy-start.16 = (f32[2240]{0:T(1024)}, f32[2240]{0:T(1024)S(1)}, u32[]{:S(2)}) copy-start(f32[2240]{0:T(1024)S(1)} %get-tuple-element.17) | copy-start | bytes 26884
  129.1 5.5 copy-start
  133.8 0.7 copy-start.5
  134.5 8.0 %copy-start.9 = (f32[70,512]{1,0:T(8,128)}, f32[70,512]{1,0:T(8,128)S(1)}, u32[]{:S(2)}) copy-start(f32[70,512]{1,0:T(8,128)S(1)} %bitcast_add_fusion) | copy-start | bytes 430084
  134.5 8.0 %copy-start.3 = (bf16[2240,1,4,128]{3,2,1,0:T(4,128)(2,1)S(1)}, bf16[2240,1,4,128]{3,2,1,0:T(4,128)(2,1)}, u32[]{:S(2)}) copy-start(bf16[2240,1,4,128]{3,2,1,0:T(4,128)(2,1)} %param.5) | copy-start | bytes 6881284
  142.5 13.2 %copy-start.1 = (bf16[2240,1,4,128]{3,2,1,0:T(4,128)(2,1)S(1)}, bf16[2240,1,4,128]{3,2,1,0:T(4,128)(2,1)}, u32[]{:S(2)}) copy-start(bf16[2240,1,4,128]{3,2,1,0:T(4,128)(2,1)} %param.7) | copy-start | bytes 6881284
  155.8 3.7 copy-start.18
  155.8 3.7 copy-start.20
  155.8 3.7 copy-start.22
  219.0 146.9 %copy-start.10 = (f32[70,512]{1,0:T(8,128)S(1)}, f32[70,512]{1,0:T(8,128)}, u32[]{:S(2)}) copy-start(f32[70,512]{1,0:T(8,128)} %copy-done.9) | copy-start | bytes 430084
  222.3 152.6 %slice-start.2 = ((s8[4587520]{0:T(1024)(128)(4,1)}), s8[393216]{0:T(1024)(128)(4,1)S(1)}, s32[]{:S(2)}) async-start(s8[4587520]{0:T(1024)(128)(4,1)} %bitcast.26), calls=%async_computation.3 | async-start | bytes 786432
  365.9 8.2 %copy-start.6 = (f32[70,1,512]{2,1,0:T(1,128)S(1)}, f32[70,1,512]{2,1,0:T(1,128)}, u32[]{:S(2)}) copy-start(f32[70,1,512]{2,1,0:T(1,128)} %copy-done.5) | copy-start | bytes 430084
  365.9 8.9 %slice-start.3 = ((s8[4587520]{0:T(1024)(128)(4,1)}), s8[4194304]{0:T(1024)(128)(4,1)S(1)}, s32[]{:S(2)}) async-start(s8[4587520]{0:T(1024)(128)(4,1)} %bitcast.26), calls=%async_computation.4 | async-start | bytes 8388608
  365.9 8.9 %copy-start.4 = (f32[70,32,32]{2,1,0:T(8,128)S(1)}, f32[70,32,32]{2,1,0:T(8,128)}, u32[]{:S(2)}) copy-start(f32[70,32,32]{2,1,0:T(8,128)} %get-tuple-element.22) | copy-start | bytes 860164
  384.2 10.9 %copy-start.7 = (pred[70,32,512]{2,1,0:T(32,128)(4,1)S(1)}, pred[70,32,512]{2,1,0:T(32,128)(4,1)}, u32[]{:S(2)}) copy-start(pred[70,32,512]{2,1,0:T(32,128)(4,1)} %gt.13) | copy-start | bytes 3440644
  384.2 10.9 %copy-start.8 = (f32[70,512]{1,0:T(8,128)S(1)}, f32[70,512]{1,0:T(8,128)}, u32[]{:S(2)}) copy-start(f32[70,512]{1,0:T(8,128)} %negate_divide_fusion) | copy-start | bytes 430084
  384.2 10.9 %copy-start.11 = (f32[70,512]{1,0:T(8,128)S(1)}, f32[70,512]{1,0:T(8,128)}, u32[]{:S(2)}) copy-start(f32[70,512]{1,0:T(8,128)} %copy-done.9) | copy-start | bytes 430084
  384.2 10.9 %copy-start.25 = (f32[70,32,32]{2,1,0:T(8,128)S(1)}, f32[70,32,32]{2,1,0:T(8,128)}, u32[]{:S(2)}) copy-start(f32[70,32,32]{2,1,0:T(8,128)} %get-tuple-element.21) | copy-start | bytes 860164
  386.8 104.2 %collective-permute-start.3 = (bf16[2240,1,1,128]{3,0,2,1:T(8,128)(2,1)}, bf16[2240,1,1,128]{3,0,2,1:T(8,128)(2,1)}, u32[]{:S(2)}, u32[]{:S(2)}) collective-permute-start(bf16[2240,1,1,128]{3,0,2,1:T(8,128)(2,1)} %copy.44), channel_id=1, source_target_pairs={{1,0},{2,1},{3,2},{5,4},{6,5},{7,6},{9,8},{10,9},{11,10},{13,12},{... | collective-permute-start | bytes 1720328 | tf_op jit(solution)/shard_map/ppermute | solution.py:18
  389.7 13.9 %slice-start = ((s8[4587520]{0:T(1024)(128)(4,1)}), s8[4194304]{0:T(1024)(128)(4,1)S(1)}, s32[]{:S(2)}) async-start(s8[4587520]{0:T(1024)(128)(4,1)} %bitcast.24), calls=%async_computation.1 | async-start | bytes 8388608
  390.6 13.0 %slice-start.1 = ((s8[4587520]{0:T(1024)(128)(4,1)}), s8[393216]{0:T(1024)(128)(4,1)S(1)}, s32[]{:S(2)}) async-start(s8[4587520]{0:T(1024)(128)(4,1)} %bitcast.24), calls=%async_computation.2 | async-start | bytes 786432
  390.6 106.1 %collective-permute-start.2 = (bf16[2240,1,1,128]{3,0,2,1:T(8,128)(2,1)}, bf16[2240,1,1,128]{3,0,2,1:T(8,128)(2,1)}, u32[]{:S(2)}, u32[]{:S(2)}) collective-permute-start(bf16[2240,1,1,128]{3,0,2,1:T(8,128)(2,1)} %copy.43), channel_id=1, source_target_pairs={{0,1},{1,2},{2,3},{4,5},{5,6},{6,7},{8,9},{9,10},{10,11},{12,13},{... | collective-permute-start | bytes 1720328 | tf_op jit(solution)/shard_map/ppermute | solution.py:17
  502.4 3.7 copy-start.13
  502.4 3.7 copy-start.15
  502.4 3.7 copy-start.17
  502.4 3.7 copy-start.19
  502.4 3.7 copy-start.21
  502.5 3.7 copy-start.23
Sparse Core Ops, SparseCore 0:
  216.6 149.2 all-reduce.4
where the time goes:
time: 562 us; the launch traced here: 555 us
  waiting for transfers between devices  139 us (25%)
  blocking collectives  130 us (23%)
  other arithmetic  118 us (21%)
  local copies, waits for them, and re-layouts  81 us (14%)
  matrix products  56.3 us (10%)
  starting transfers between devices  16.3 us (3%)
  between operations  14.7 us (3%)
    psum x1, waiting for transfers between devices, shards(): state, key_sum = lax.psum((local_state, local_sum), ('frame', 'row'))  139 us
    psum x1, blocking collectives, shards(): state, key_sum = lax.psum((local_state, local_sum), ('frame', 'row'))  65.3 us
    psum x1, blocking collectives, shards(): lax.psum((local_gstate, local_gsum), ('frame', 'row'))  64.3 us
    convert_element_type x1, other arithmetic, shards(): conv_taps(pad_columns(grad_ext), weights, True, row_count, col_count)  41.7 us
    add x1, other arithmetic, conv_taps(): summed = tap_term if summed is None else summed + tap_term  41.7 us
    reduce_sum x1, other arithmetic, shards(): local_sum = jnp.sum(key_act, axis=2)  18 us
    ppermute x2, local copies, waits for them, and re-layouts, extended(): before = lax.ppermute(last, axis, up)  11.7 us
    ppermute x2, local copies, waits for them, and re-layouts, extended(): after = lax.ppermute(leading, axis, down)  11.4 us
  transfers between devices with their start and end apart: 5, of which 1 were waited for; matrix products, arithmetic and copies ran while one was open for 20% of the time, Pallas kernels for 0%

commit v1 on v0

--- a/solution.py
+++ b/solution.py
@@ -65,7 +65,11 @@
     grad_den = -jnp.sum(grad_out * output, axis=1) / denom
     local_gstate = jnp.einsum("hjt,het->hje", query_act, grad_num, precision=highest)
     local_gsum = jnp.einsum("hjt,ht->hj", query_act, grad_den, precision=highest)
-    grad_state, grad_sum = lax.psum((local_gstate, local_gsum), ("frame", "row"))
+
+    def fill_slices(panel, axis_name, axis_id):
+        return jax.lax.psum(jax.lax.psum(panel, axis_name), axis_id)
+
+    grad_state, grad_sum = fill_slices((local_gstate, local_gsum), "row", "frame")
     grad_qact = (
         jnp.einsum("hje,het->hjt", state, grad_num, precision=highest)
         + key_sum[:, :, None] * grad_den[:, None, :]

time: 562 us -> 971 us (1.73)
  the two profiles are of different devices: /device:TPU:1 before, /device:TPU:0 now
where the time goes in v1:
time: 971 us; the launch traced here: 966 us
  waiting for transfers between devices  474 us (49%)
  blocking collectives  239 us (25%)
  other arithmetic  97.2 us (10%)
  local copies, waits for them, and re-layouts  75.7 us (8%)
  matrix products  58.4 us (6%)
  between operations  14.3 us (1%)
    psum x2, waiting for transfers between devices, fill_slices(): return jax.lax.psum(jax.lax.psum(panel, axis_name), axis_id)  334 us
    psum x2, blocking collectives, fill_slices(): return jax.lax.psum(jax.lax.psum(panel, axis_name), axis_id)  170 us
    psum x1, waiting for transfers between devices, shards(): state, key_sum = lax.psum((local_state, local_sum), ('frame', 'row'))  140 us
    psum x1, blocking collectives, shards(): state, key_sum = lax.psum((local_state, local_sum), ('frame', 'row'))  68.6 us
    convert_element_type x1, other arithmetic, shards(): conv_taps(pad_columns(grad_ext), weights, True, row_count, col_count)  61.2 us
  transfers between devices with their start and end apart: 7, of which 3 were waited for; matrix products, arithmetic and copies ran while one was open for 6% of the time, Pallas kernels for 0%

profile of v1, /device:TPU:0, one launch (start us, length us, event | category | flops | bytes accessed | tf_op | source)
XLA Modules:
  0.0 966.2 jit_solution(356597379997661655)
XLA Ops:
  7.2 0.0 all-reduce.8.cloned.1.call-start
  7.2 4.6 convert_maximum_fusion
  11.8 6.5 reshape.168
  18.3 0.0 copy-done
  18.3 17.9 %fusion.30 = (f32[2240]{0:T(1024)S(1)}, f32[2240,1,4,128]{3,2,1,0:T(4,128)}) fusion(bf16[2240,1,4,128]{3,2,1,0:T(4,128)(2,1)S(1)} %copy-done), kind=kLoop, calls=%fused_computation.59 | loop fusion | flops 3438400 | bytes 6890240 | tf_op jit(solution)/shard_map/reduce_sum | solution.py:55
  36.2 0.1 reduce_sum.21
  36.2 68.6 %psum.43 = f32[70,32]{1,0:T(8,128)S(1)} all-reduce(f32[70,32]{1,0:T(8,128)S(1)} %reduce_sum.21), channel_id=1, replica_groups=mesh['frame'=32,'row'=4] {'frame','row'}, use_global_device_ids=true, to_apply=%region_2.3 | all-reduce | flops 2240 | bytes 17920 | tf_op jit(solution)/shard_map/psum | solution.py:56
  104.9 4.6 fusion.33
  109.5 0.6 copy-done.7
  110.2 0.0 copy-done.6
  110.2 2.8 reshape.172
  113.0 9.3 fusion.29
  122.3 0.0 all-reduce.8.cloned.1.call-update
  122.3 0.0 all-reduce.10.cloned.1.call-start
  122.4 42.4 %all-reduce.8.cloned.1.call-done = f32[70,32,32]{2,1,0:T(8,128)} async-done(((f32[70,32,32]{2,1,0:T(8,128)}), f32[70,32,32]{2,1,0:T(8,128)}) %all-reduce.8.cloned.1.call-update) | async-done | bytes 286736 | tf_op jit(solution)/shard_map/psum | solution.py:70
  164.8 0.0 all-reduce.10.cloned.1.call-update
  164.8 0.0 all-reduce.6.cloned.1.call-start
  164.9 1.7 fusion.36
  166.6 0.9 copy.41
  167.4 3.1 collective-permute-start
  170.5 0.9 copy.42
  171.4 1.5 collective-permute-start.1
  172.9 6.3 reshape.164
  179.2 291.7 %all-reduce.10.cloned.1.call-done = f32[70,32,32]{2,1,0:T(8,128)} async-done(((f32[70,32,32]{2,1,0:T(8,128)}), f32[70,32,32]{2,1,0:T(8,128)}) %all-reduce.10.cloned.1.call-update) | async-done | bytes 286736 | tf_op jit(solution)/shard_map/psum | solution.py:70
  471.0 7.2 convolution_convert_fusion
  478.2 4.1 convert_element_type.73
  482.3 0.0 copy-start.1
  482.3 1.7 fusion.35
  484.0 0.0 copy-start.13
  484.0 0.1 copy.43
  484.1 0.0 copy-start.3
  484.1 1.5 collective-permute-start.2
  485.5 0.1 copy.44
  485.6 1.3 collective-permute-start.3
  486.9 1.5 broadcast_compare_fusion
  488.5 0.2 slice_reduce_fusion.8
  488.7 0.0 collective-permute-done
  488.8 5.7 copy.24
  494.5 0.0 collective-permute-done.1
  494.5 5.7 copy.25
  500.2 3.6 maximum_convert_fusion
  503.9 0.0 collective-permute-done.2
  503.9 9.3 copy.30
  513.2 0.0 collective-permute-done.3
  513.2 9.3 copy.32
  522.5 5.7 maximum_convert_fusion.1
  528.2 61.2 %fusion.28 = (bf16[2240,1,4,128]{3,2,1,0:T(4,128)(2,1)}, f32[2240,1,4,128]{3,2,1,0:T(4,128)}) fusion(f32[2240,1,6,128]{3,2,1,0:T(8,128)} %maximum_convert_fusion.1, f32[2240]{0:T(1024)S(1)} %get-tuple-element.13, f32[2240]{0:T(1024)S(1)} %get-tuple-element.14, f32[2240]{0:T(1024)S(1)} %get-tuple-element.15, f32[2240]{0:T(1024)S(1)} %get-tuple-element.16, ...), kind=kLoop, calls=%fused_computation.53 | loop fusion | flops 40140800 | bytes 52867072 | tf_op jit(solution)/shard_map/convert_element_type | solution.py:93
  589.4 6.7 reshape.165
  596.1 0.0 copy-start.4
  596.2 9.1 fusion.37
  605.3 0.0 all-reduce.6.cloned.1.call-update
  605.3 2.5 broadcast_compare_fusion.1
  607.8 3.3 gt.15
  611.1 5.6 gt.13
  616.7 140.1 %all-reduce.6.cloned.1.call-done = f32[70,32,32]{2,1,0:T(8,128)} async-done(((f32[70,32,32]{2,1,0:T(8,128)}), f32[70,32,32]{2,1,0:T(8,128)}) %all-reduce.6.cloned.1.call-update) | async-done | bytes 286736 | tf_op jit(solution)/shard_map/psum | solution.py:56
  756.8 7.6 multiply_reduce_fusion
  764.5 5.9 fusion.31
  770.4 15.3 %psum.46 = f32[70,32]{1,0:T(8,128)S(1)} all-reduce(f32[70,32]{1,0:T(8,128)S(1)} %bitcast.28), channel_id=1, replica_groups=mesh['frame'=32,'row'=4] {'row'}, use_global_device_ids=true, to_apply=%region_6.7 | all-reduce | flops 2240 | bytes 17920 | tf_op jit(solution)/shard_map/psum | solution.py:70
  785.7 154.9 %psum.47 = f32[70,32]{1,0:T(8,128)S(1)} all-reduce(f32[70,32]{1,0:T(8,128)S(1)} %psum.46), channel_id=1, replica_groups=mesh['frame'=32,'row'=4] {'frame'}, use_global_device_ids=true, to_apply=%region_7.8 | all-reduce | flops 2240 | bytes 17920 | tf_op jit(solution)/shard_map/psum | solution.py:70
  940.6 7.2 select_convert_fusion
  947.8 0.0 copy-start.9
  947.8 2.1 reshape.170
  949.9 7.5 select_convert_fusion.1
  957.3 2.1 reshape.169
  (24 shorter events, 0.1 us)
Async XLA Ops:
  7.2 157.6 %all-reduce.8.cloned.1.call-start = ((), (), s32[]{:S(2)}) async-start(), calls=%async_computation.1 | async-start | bytes 2293760 | tf_op jit(solution)/shard_map/psum | solution.py:70
  11.8 6.5 copy-start
  36.2 74.0 %copy-start.6 = (bf16[2240,1,4,128]{3,2,1,0:T(4,128)(2,1)S(1)}, bf16[2240,1,4,128]{3,2,1,0:T(4,128)(2,1)}, u32[]{:S(2)}) copy-start(bf16[2240,1,4,128]{3,2,1,0:T(4,128)(2,1)} %param.8) | copy-start | bytes 6881284
  109.5 0.6 copy-start.7
  110.2 12.1 %copy-start.11 = (f32[70,512]{1,0:T(8,128)}, f32[70,512]{1,0:T(8,128)S(1)}, u32[]{:S(2)}) copy-start(f32[70,512]{1,0:T(8,128)S(1)} %bitcast_add_fusion) | copy-start | bytes 430084
  113.0 51.9 %copy-start.2 = (bf16[2240,1,4,128]{3,2,1,0:T(4,128)(2,1)S(1)}, bf16[2240,1,4,128]{3,2,1,0:T(4,128)(2,1)}, u32[]{:S(2)}) copy-start(bf16[2240,1,4,128]{3,2,1,0:T(4,128)(2,1)} %param.7) | copy-start | bytes 6881284
  122.3 348.6 %all-reduce.10.cloned.1.call-start = ((), (), s32[]{:S(2)}) async-start(), calls=%async_computation.2 | async-start | bytes 2293760 | tf_op jit(solution)/shard_map/psum | solution.py:70
  164.8 592.0 %all-reduce.6.cloned.1.call-start = ((), (), s32[]{:S(2)}) async-start(), calls=%async_computation | async-start | bytes 2293760 | tf_op jit(solution)/shard_map/psum | solution.py:56
  167.4 321.3 %collective-permute-start = (bf16[2240,1,1,128]{3,0,2,1:T(8,128)(2,1)}, bf16[2240,1,1,128]{3,0,2,1:T(8,128)(2,1)}, u32[]{:S(2)}, u32[]{:S(2)}) collective-permute-start(bf16[2240,1,1,128]{3,0,2,1:T(8,128)(2,1)} %copy.41), channel_id=1, source_target_pairs={{0,1},{1,2},{2,3},{4,5},{5,6},{6,7},{8,9},{9,10},{10,11},{12,13},{... | collective-permute-start | bytes 1720328 | tf_op jit(solution)/shard_map/ppermute | solution.py:17
  171.4 323.0 %collective-permute-start.1 = (bf16[2240,1,1,128]{3,0,2,1:T(8,128)(2,1)}, bf16[2240,1,1,128]{3,0,2,1:T(8,128)(2,1)}, u32[]{:S(2)}, u32[]{:S(2)}) collective-permute-start(bf16[2240,1,1,128]{3,0,2,1:T(8,128)(2,1)} %copy.42), channel_id=1, source_target_pairs={{1,0},{2,1},{3,2},{5,4},{6,5},{7,6},{9,8},{10,9},{11,10},{13,12},{... | collective-permute-start | bytes 1720328 | tf_op jit(solution)/shard_map/ppermute | solution.py:18
  482.3 4.6 copy-start.1
  484.0 4.5 copy-start.13
  484.1 16.2 %copy-start.3 = (bf16[2240,1,4,128]{3,2,1,0:T(4,128)(2,1)S(1)}, bf16[2240,1,4,128]{3,2,1,0:T(4,128)(2,1)}, u32[]{:S(2)}) copy-start(bf16[2240,1,4,128]{3,2,1,0:T(4,128)(2,1)} %param.7) | copy-start | bytes 6881284
  484.1 19.8 %collective-permute-start.2 = (bf16[2240,1,1,128]{3,0,2,1:T(8,128)(2,1)S(1)}, bf16[2240,1,1,128]{3,0,2,1:T(8,128)(2,1)S(1)}, u32[]{:S(2)}, u32[]{:S(2)}) collective-permute-start(bf16[2240,1,1,128]{3,0,2,1:T(8,128)(2,1)S(1)} %copy.43), channel_id=1, source_target_pairs={{0,1},{1,2},{2,3},{4,5},{5,6},{6,7},{8,9},{9,10},{10,11},{12,13},{... | collective-permute-start | bytes 1720328 | tf_op jit(solution)/shard_map/ppermute | solution.py:17
  485.6 27.5 %collective-permute-start.3 = (bf16[2240,1,1,128]{3,0,2,1:T(8,128)(2,1)S(1)}, bf16[2240,1,1,128]{3,0,2,1:T(8,128)(2,1)S(1)}, u32[]{:S(2)}, u32[]{:S(2)}) collective-permute-start(bf16[2240,1,1,128]{3,0,2,1:T(8,128)(2,1)S(1)} %copy.44), channel_id=1, source_target_pairs={{1,0},{2,1},{3,2},{5,4},{6,5},{7,6},{9,8},{10,9},{11,10},{13,12},{... | collective-permute-start | bytes 1720328 | tf_op jit(solution)/shard_map/ppermute | solution.py:18
  596.1 9.1 copy-start.4
  607.8 149.0 %copy-start.12 = (f32[70,512]{1,0:T(8,128)S(1)}, f32[70,512]{1,0:T(8,128)}, u32[]{:S(2)}) copy-start(f32[70,512]{1,0:T(8,128)} %copy-done.11) | copy-start | bytes 430084
  616.7 147.7 %copy-start.8 = (f32[70,1,512]{2,1,0:T(1,128)S(1)}, f32[70,1,512]{2,1,0:T(1,128)}, u32[]{:S(2)}) copy-start(f32[70,1,512]{2,1,0:T(1,128)} %copy-done.7) | copy-start | bytes 430084
  764.4 176.2 %copy-start.5 = (pred[70,32,512]{2,1,0:T(32,128)(4,1)S(1)}, pred[70,32,512]{2,1,0:T(32,128)(4,1)}, u32[]{:S(2)}) copy-start(pred[70,32,512]{2,1,0:T(32,128)(4,1)} %gt.15) | copy-start | bytes 3440644
  764.5 21.2 %copy-start.10 = (f32[70,512]{1,0:T(8,128)}, f32[70,512]{1,0:T(8,128)S(1)}, u32[]{:S(2)}) copy-start(f32[70,512]{1,0:T(8,128)S(1)} %negate_divide_fusion) | copy-start | bytes 430084
  947.8 2.1 copy-start.9
Sparse Core Ops, SparseCore 0:
  122.4 42.3 all-reduce.7
  167.3 303.6 all-reduce.9
  605.4 151.3 all-reduce.5
